TPU v7x, 32 devices: a whole 2x2x4 slice. The times are simulated.
32 devices in a mesh: grp: 4 (over y, x), blk: 8 (over z, core).
Axes of the slice: x: 2, y: 2, z: 4, core: 2. Of those that a mesh axis runs over, the one named last changes fastest.
Arguments:
- activations: bfloat16 [32768, 3072], P(('grp', 'blk')), may hold values from -6 to 6
- out_grads: bfloat16 [32768, 3072], P(('grp', 'blk')), may hold values from -6 to 6
- proj_act: bfloat16 [3072, 128], replicated, may hold values from -1 to 1
- proj_out: bfloat16 [3072, 256], replicated, may hold values from -0.109375 to 0.109375
Outputs:
- scores: float32 [512, 128], P(('grp', 'blk'))
All inputs are finite; a program needn't handle non-finite values.
Results may differ from a plain program's by a relative error of at most 0.0012.
Values may be sent and summed in bfloat16 or wider, within the bound.
A program may use at most 128 MiB of HBM per device.

v0:
```python
import math

import jax
import jax.numpy as jnp
from jax import lax
from jax.sharding import PartitionSpec as P

SEQ = 64
ITERS = 4


damping_rate = 0.5
power_steps = 3


def top_estimate(gram_sum):
    width = gram_sum.shape[0]
    vector = jnp.full((width,), 1.0 / math.sqrt(width), jnp.float32)
    top = jnp.float32(1.0)
    for step in range(power_steps):
        image = jnp.dot(gram_sum, vector, precision=lax.Precision.HIGHEST)
        top = jnp.sqrt(jnp.sum(image * image) + 1e-06)
        vector = image / top
    return top


def chebyshev(gram_sum, damping, right_side):
    radius = top_estimate(gram_sum)
    center = damping + radius

    def operate(field):
        return jnp.dot(gram_sum, field, precision=lax.Precision.HIGHEST) + damping * field

    stride = 1.0 / center
    direction = right_side
    solution = stride * direction
    residual = right_side - stride * operate(direction)
    for sweep in range(1, ITERS):
        if sweep == 1:
            momentum = 0.5 * (radius * stride) ** 2
        else:
            momentum = (0.5 * radius * stride) ** 2
        stride = 1.0 / (center - momentum / stride)
        direction = residual + momentum * direction
        solution = solution + stride * direction
        if sweep + 1 < ITERS:
            residual = residual - stride * operate(direction)
    return solution


def self_product(rows):
    return lax.dot_general(rows, rows, (((0,), (0,)), ((), ())), preferred_element_type=jnp.float32)


def shards(activations, out_grads, proj_act, proj_out):
    examples = activations.shape[0] // SEQ
    act_low = jnp.dot(activations, proj_act, preferred_element_type=jnp.float32).astype(
        jnp.bfloat16
    )
    grad_low = jnp.dot(out_grads, proj_out, preferred_element_type=jnp.float32).astype(jnp.bfloat16)
    features = jnp.einsum(
        "etr,ets->ers",
        act_low.reshape(examples, SEQ, -1),
        grad_low.reshape(examples, SEQ, -1),
        preferred_element_type=jnp.float32,
    )
    features = features.astype(jnp.bfloat16).reshape(examples, -1)
    block_rows = lax.all_to_all(features, "blk", split_axis=1, concat_axis=0, tiled=True)
    width = block_rows.shape[1]
    gram_sum = self_product(lax.all_gather(block_rows, "grp", axis=0, tiled=True))
    total = lax.psum(jnp.trace(gram_sum), "blk")
    damping = damping_rate * total / (width * lax.axis_size("blk"))
    right_side = block_rows.T.astype(jnp.float32)
    solved = chebyshev(gram_sum, damping, right_side).astype(jnp.bfloat16)
    scores = lax.psum_scatter(
        jnp.dot(block_rows, solved, preferred_element_type=jnp.float32),
        "blk",
        scatter_dimension=0,
        tiled=True,
    )
    return scores * float(examples * lax.axis_size("grp"))


def solution(mesh):
    in_specs = (P(("grp", "blk"), None), P(("grp", "blk"), None), P(), P())
    out_specs = P(("grp", "blk"), None)
    return jax.shard_map(shards, mesh=mesh, in_specs=in_specs, out_specs=out_specs, check_vma=False)
```

profile of v0, /device:TPU:0, one launch (start us, length us, event | category | flops | bytes accessed | tf_op | source)
XLA Modules:
  0.0 536.7 jit_solution(3216748590746869479)
XLA Ops:
  6.5 4.9 convolution_convert_fusion.2
  11.4 0.4 copy-done.4
  11.8 1.8 convolution_convert_fusion.1
  13.6 0.5 convolution_convert_fusion
  14.1 1.3 all_to_all.14
  15.5 1.8 copy.6
  17.3 32.8 %all_to_all.19 = bf16[16,8,4096]{2,0,1:T(8,128)(2,1)} all-to-all(bf16[16,8,4096]{2,0,1:T(8,128)(2,1)S(1)} %copy.6), channel_id=1, replica_groups=mesh['grp'=4,'blk'=8] {'blk'}, dimensions={1} | all-to-all | bytes 2097152 | tf_op jit(solution)/shard_map/all_to_all | solution.py:68
  50.1 0.3 reduce-scatter.2.cloned.1.call-start
  50.4 2.3 copy.7
  52.7 49.1 %all-gather.2.cloned.1.call-done = bf16[512,4096]{1,0:T(8,128)(2,1)} async-done(((bf16[128,4096]{1,0:T(8,128)(2,1)}), bf16[512,4096]{1,0:T(8,128)(2,1)}) %all-gather.2.cloned.1.call-update) | async-done | bytes 4194320 | tf_op jit(solution)/shard_map/all_gather | solution.py:70
  101.8 37.9 %select_reduce_fusion = (f32[]{:T(128)}, f32[4096,4096]{1,0:T(8,128)}) fusion(bf16[512,4096]{1,0:T(8,128)(2,1)} %all-gather.2.cloned.1.call-done), kind=kOutput, calls=%fused_computation | convolution fusion | flops 17230200832 | bytes 71303168 | tf_op jit(solution)/shard_map/dot_general | solution.py:52
  139.7 17.1 %psum.7 = f32[]{:T(128)} all-reduce(f32[]{:T(128)} %get-tuple-element.5), channel_id=1, replica_groups=mesh['grp'=4,'blk'=8] {'blk'}, use_global_device_ids=true, to_apply=%region_1.2 | all-reduce | flops 1 | bytes 8 | tf_op jit(solution)/shard_map/psum | solution.py:71
  156.8 60.2 %fusion.21 = f32[1,4096]{1,0:T(1,128)S(1)} fusion(f32[4096,4096]{1,0:T(8,128)} %get-tuple-element.6), kind=kOutput, calls=%fused_computation.33 | convolution fusion | flops 201326592 | bytes 67125248 | tf_op jit(solution)/shard_map/dot_general | solution.py:21
  217.0 0.6 multiply_reduce_fusion.2
  218.2 59.9 %fusion.24 = f32[1,4096]{1,0:T(1,128)S(1)} fusion(f32[4096,4096]{1,0:T(8,128)} %get-tuple-element.6, f32[4096,1]{0,1:T(1,128)S(1)} %bitcast.77), kind=kOutput, calls=%fused_computation.39 | convolution fusion | flops 201326592 | bytes 67141632 | tf_op jit(solution)/shard_map/dot_general | solution.py:21
  278.1 0.6 multiply_reduce_fusion.1
  279.3 60.4 %fusion.25 = f32[1,4096]{1,0:T(1,128)S(1)} fusion(f32[4096,4096]{1,0:T(8,128)} %get-tuple-element.6, f32[4096,1]{0,1:T(1,128)S(1)} %bitcast.78), kind=kOutput, calls=%fused_computation.40 | convolution fusion | flops 201326592 | bytes 67141632 | tf_op jit(solution)/shard_map/dot_general | solution.py:21
  339.7 0.6 multiply_reduce_fusion
  341.7 36.6 %fusion.3 = f32[4096,128]{1,0:T(8,128)} fusion(f32[4096,4096]{1,0:T(8,128)} %get-tuple-element.6, bf16[128,4096]{1,0:T(8,128)(2,1)S(1)} %bitcast.68, bf16[128,4096]{0,1:T(8,128)(2,1)} %copy.7, f32[]{:T(128)S(6)} %div.36, f32[]{:T(128)S(6)} %div.41), kind=kOutput, calls=%fused_computation.8 | convolution fusion | flops 25772425216 | bytes 71303176 | tf_op jit(solution)/shard_map/dot_general | solution.py:32
  378.4 61.5 %fusion.4 = f32[4096,128]{1,0:T(8,128)S(1)} fusion(f32[4096,128]{1,0:T(8,128)} %fusion.3, f32[4096,4096]{1,0:T(8,128)} %get-tuple-element.6, bf16[128,4096]{0,1:T(8,128)(2,1)} %copy.7, f32[]{:T(128)S(6)} %mul.106, f32[]{:T(128)S(6)} %div.36, f32[]{:T(128)S(6)} %div.43), kind=kOutput, calls=%fused_computation.9 | convolution fusion | flops 25775046656 | bytes 72351760 | tf_op jit(solution)/shard_map/dot_general | solution.py:32
  439.9 59.5 %fusion.9 = bf16[4096,128]{1,0:T(8,128)(2,1)S(1)} fusion(f32[4096,128]{1,0:T(8,128)S(1)} %fusion.4, f32[4096,4096]{1,0:T(8,128)} %get-tuple-element.6, bf16[128,4096]{0,1:T(8,128)(2,1)S(1)} %copy-done.3, f32[4096,128]{1,0:T(8,128)S(1)} %copy-done.2, f32[]{:T(128)S(6)} %integer_pow.11, f32[]{:T(128)S(6)} %div.47, f32[]{:T(128)S(6)} %integer_pow.10, ...), kind=kOutput, calls=%fused_computation.14 | convolution fusion | flops 25782386688 | bytes 73400352 | tf_op jit(solution)/shard_map/dot_general | solution.py:32
  499.4 1.1 fusion.26
  500.5 27.9 %reduce-scatter.2.cloned.1.call-done = f32[16,128]{1,0:T(8,128)} async-done(((f32[128,128]{1,0:T(8,128)}), f32[16,128]{1,0:T(8,128)}) %reduce-scatter.2.cloned.1.call-update) | async-done | bytes 8208 | tf_op jit(solution)/shard_map/reduce_scatter | solution.py:75
  528.4 1.3 broadcast_multiply_fusion
  (14 shorter events, 0.1 us)
Async XLA Ops:
  6.5 4.9 copy-start
  6.5 95.2 %all-gather.2.cloned.1.call-start = ((), (), s32[]{:S(2)}) async-start(), calls=%async_computation.2 | async-start | bytes 5242880 | tf_op jit(solution)/shard_map/all_gather | solution.py:70
  6.5 5.3 copy-start.4
  50.1 478.3 %reduce-scatter.2.cloned.1.call-start = ((), (), s32[]{:S(2)}) async-start(), calls=%async_computation.3 | async-start | bytes 73728 | tf_op jit(solution)/shard_map/reduce_scatter | solution.py:75
  279.3 62.4 %copy-start.1 = (bf16[16,8,4096]{2,0,1:T(8,128)(2,1)S(1)}, bf16[16,8,4096]{2,0,1:T(8,128)(2,1)}, u32[]{:S(2)}) copy-start(bf16[16,8,4096]{2,0,1:T(8,128)(2,1)} %all_to_all.19) | copy-start | bytes 3145732
  378.4 61.5 %copy-start.2 = (f32[4096,128]{1,0:T(8,128)S(1)}, f32[4096,128]{1,0:T(8,128)}, u32[]{:S(2)}) copy-start(f32[4096,128]{1,0:T(8,128)} %fusion.3) | copy-start | bytes 6291460
  378.4 61.5 %copy-start.3 = (bf16[128,4096]{0,1:T(8,128)(2,1)S(1)}, bf16[128,4096]{0,1:T(8,128)(2,1)}, u32[]{:S(2)}) copy-start(bf16[128,4096]{0,1:T(8,128)(2,1)} %copy.7) | copy-start | bytes 3145732
Sparse Core Ops, SparseCore 0:
  50.2 51.4 all-gather.1
  500.7 27.6 reduce-scatter.1
where the time goes:
time: 541 us; the launch traced here: 537 us
  matrix products  384 us (71%)
  waiting for transfers between devices  77 us (14%)
  blocking collectives  49.9 us (9%)
  between operations  16.4 us (3%)
  local copies, waits for them, and re-layouts  5.84 us (1%)
    dot_general x3, matrix products, top_estimate(): image = jnp.dot(gram_sum, vector, precision=lax.Precision.HIGHEST)  180 us
    dot_general x3, matrix products, operate(): jnp.dot(gram_sum, field, precision=lax.Precision.HIGHEST) + damping * field  158 us
    all_gather x1, waiting for transfers between devices, shards(): lax.all_gather(block_rows, 'grp', axis=0, tiled=True)  49.1 us
    dot_general x1, matrix products, self_product(): lax.dot_general(rows, rows, (((0,), (0,)), ((), ())), preferred_element_t...  37.9 us
    all_to_all x1, blocking collectives, shards(): lax.all_to_all(features, 'blk', split_axis=1, concat_axis=0, tiled=True)  32.8 us
    reduce_scatter x1, waiting for transfers between devices, shards(): lax.psum_scatter(jnp.dot(block_rows, solved, preferred_element_type=jnp.f...  27.9 us
    psum x1, blocking collectives, shards(): total = lax.psum(jnp.trace(gram_sum), 'blk')  17.1 us
  transfers between devices with their start and end apart: 2, of which 2 were waited for; matrix products, arithmetic and copies ran while one was open for 0% of the time, Pallas kernels for 0%

commit v1 on v0

v1 whole, which is shorter than its diff:
```python
import functools
import math

import jax
import jax.numpy as jnp
from jax import lax
from jax.experimental import pallas as pl
from jax.experimental.pallas import tpu as pltpu
from jax.sharding import PartitionSpec as P

SEQ = 64
ITERS = 4
damping_rate = 0.5
power_steps = 3
MESH = pl.DeviceIdType.MESH
NT = (((1,), (1,)), ((), ()))
TN = (((0,), (0,)), ((), ()))


def feature_kernel(examples, act_ref, grad_ref, feat_ref, stat_ref, wide):
    rank = act_ref.shape[1]
    for e in range(examples):
        tokens = pl.ds(e * SEQ, SEQ)
        product = lax.dot_general(
            act_ref[tokens, :], grad_ref[tokens, :], TN, preferred_element_type=jnp.float32
        )
        for c in range(wide.shape[0]):
            wide[c, pl.ds(e, rank, stride=examples), :] = product[:, c * 128:(c + 1) * 128]

    def step(i, acc):
        rows = pl.ds(pl.multiple_of(i * 128, 128), 128)
        for c in range(wide.shape[0]):
            low = wide[c, rows, :].astype(jnp.bfloat16)
            feat_ref[rows, c * 128:(c + 1) * 128] = low
            back = low.astype(jnp.float32)
            acc += back * back
        return acc

    acc = lax.fori_loop(0, wide.shape[1] // 128, step, jnp.zeros((128, 128), jnp.float32))
    stat_ref[...] = jnp.broadcast_to(jnp.sum(acc, keepdims=True), stat_ref.shape)


def mix_kernel(
    groups, blocks, examples, ranks, width,
    feat_ref, stat_ref, out_ref,
    recv, stats, part, landed, full, prow_part, prow_land, row, col, col_next,
    y_ref, sc, sc_land,
    f_send, f_recv, t_send, t_recv, r_send, r_recv, g_send, g_recv, p_send, p_recv, s_send, s_recv,
):
    devices = groups * blocks
    group_ex = examples * blocks
    total_ex = group_ex * groups
    span = recv.shape[2]
    rows_out = ranks * examples
    grp, blk = lax.axis_index("grp"), lax.axis_index("blk")
    me = grp * blocks + blk

    def peer_of(d):
        peer = lax.rem(me + d, devices)
        return peer, peer // blocks, lax.rem(peer, blocks)

    barrier = pltpu.get_barrier_semaphore()

    def greet(d, c):
        _, pg, pb = peer_of(d)
        pl.semaphore_signal(barrier, inc=1, device_id=(pg, pb), device_id_type=MESH)
        return c

    lax.fori_loop(1, devices, greet, 0)
    pl.semaphore_wait(barrier, devices - 1)

    def feature_copy(dest, pg, pb, slot):
        start = pl.multiple_of((pb * groups + pg) * rows_out, rows_out)
        return pltpu.make_async_remote_copy(
            src_ref=feat_ref.at[pl.ds(start, rows_out)], dst_ref=recv.at[slot],
            send_sem=f_send.at[dest], recv_sem=f_recv.at[slot],
            device_id=(pg, pb), device_id_type=MESH)

    def stat_copy(dest, pg, pb, slot):
        return pltpu.make_async_remote_copy(
            src_ref=stat_ref, dst_ref=stats.at[slot],
            send_sem=t_send.at[dest], recv_sem=t_recv.at[slot],
            device_id=(pg, pb), device_id_type=MESH)

    def send(d, c):
        peer, pg, pb = peer_of(d)
        feature_copy(peer, pg, pb, me).start()
        return c

    lax.fori_loop(1, devices, send, 0)

    def send_stat(d, c):
        peer, pg, pb = peer_of(d)
        stat_copy(peer, pg, pb, me).start()
        return c

    lax.fori_loop(1, devices, send_stat, 0)
    own = pl.multiple_of((blk * groups + grp) * rows_out, rows_out)
    recv[me] = feat_ref[pl.ds(own, rows_out), :]
    stats[me] = stat_ref[...]

    def arrive(d, c):
        peer, pg, pb = peer_of(d)
        feature_copy(peer, pg, pb, peer).wait_recv()
        return c

    lax.fori_loop(1, devices, arrive, 0)

    def grp_rows(h):
        return pl.ds(pl.multiple_of(h * group_ex, group_ex), group_ex)

    def part_rows(h):
        for r in range(ranks):
            here = pl.ds(r * examples, examples)
            left = recv[pl.ds(h * blocks, blocks), here, :].reshape(group_ex, span)
            for c in range(groups):
                right = recv[c * blocks:(c + 1) * blocks, here, :].reshape(group_ex, span)
                term = lax.dot_general(left, right, NT, preferred_element_type=jnp.float32)
                cols = slice(c * group_ex, (c + 1) * group_ex)
                if r == 0:
                    part[grp_rows(h), cols] = term
                else:
                    part[grp_rows(h), cols] += term

    def part_copy(h, slot):
        return pltpu.make_async_remote_copy(
            src_ref=part.at[grp_rows(h)], dst_ref=landed.at[slot],
            send_sem=r_send.at[h], recv_sem=r_recv.at[slot],
            device_id=(h, blk), device_id_type=MESH)

    def full_copy(h, slot):
        return pltpu.make_async_remote_copy(
            src_ref=full.at[grp_rows(slot)], dst_ref=full.at[grp_rows(slot)],
            send_sem=g_send.at[h], recv_sem=g_recv.at[slot],
            device_id=(h, blk), device_id_type=MESH)

    def prow_copy(h, slot):
        return pltpu.make_async_remote_copy(
            src_ref=prow_part, dst_ref=prow_land.at[slot],
            send_sem=p_send.at[h], recv_sem=p_recv.at[slot],
            device_id=(h, blk), device_id_type=MESH)

    others = [lax.rem(grp + d, groups) for d in range(1, groups)]

    def part_step(d, c):
        h = lax.rem(grp + d, groups)
        part_rows(h)
        part_copy(h, grp).start()
        return c

    lax.fori_loop(1, groups, part_step, 0)
    part_rows(grp)

    ones = jnp.ones((8, span), jnp.bfloat16)
    scale = 1.0 / math.sqrt(width)
    for c in range(groups):
        cols = slice(c * group_ex, (c + 1) * group_ex)
        acc = jnp.zeros((8, group_ex), jnp.float32)
        for r in range(ranks):
            right = recv[c * blocks:(c + 1) * blocks, pl.ds(r * examples, examples), :]
            acc += lax.dot_general(
                ones, right.reshape(group_ex, span), NT, preferred_element_type=jnp.float32)
        prow_part[:, cols] = acc * scale
    for h in others:
        prow_copy(h, grp).start()

    for h in others:
        part_copy(h, h).wait_recv()
    mine = part[grp_rows(grp), :]
    for h in others:
        mine += landed[h]
    full[grp_rows(grp), :] = mine
    for h in others:
        full_copy(h, grp).start()

    def arrive_stat(d, c):
        peer, pg, pb = peer_of(d)
        stat_copy(peer, pg, pb, peer).wait_recv()
        return c

    lax.fori_loop(1, devices, arrive_stat, 0)
    total = jnp.sum(stats[...], axis=0)[:1, :1]
    damping = damping_rate * total / (width * blocks)
    for h in others:
        prow_copy(h, h).wait_recv()
    first = prow_part[...]
    for h in others:
        first += prow_land[h]
    row[...] = first
    for h in others:
        full_copy(h, h).wait_recv()

    tile = 128
    tiles = total_ex // tile

    def tile_rows(i):
        return pl.ds(pl.multiple_of(i * tile, tile), tile)

    def turn(i, c):
        spot = lax.broadcasted_iota(jnp.int32, (tile, total_ex), 0) + i * tile
        lane = lax.broadcasted_iota(jnp.int32, (tile, total_ex), 1)
        picked = jnp.where(spot == lane, row[:1, :], 0.0)
        col[tile_rows(i), :] = jnp.broadcast_to(
            jnp.sum(picked, axis=1, keepdims=True), (tile, 128))
        return c

    lax.fori_loop(0, tiles, turn, 0)
    top = None
    for step in range(power_steps):
        last = step + 1 == power_steps
        prow = row[:1, :]

        def image(i, acc):
            k_tile = full[tile_rows(i), :]
            if not last:
                col_next[tile_rows(i), :] = jnp.broadcast_to(
                    jnp.sum(k_tile * prow, axis=1, keepdims=True), (tile, 128))
            return acc + jnp.sum(k_tile * col[tile_rows(i), :][:, :1], axis=0, keepdims=True)

        q = lax.fori_loop(0, tiles, image, jnp.zeros((1, total_ex), jnp.float32))
        square = jnp.sum(prow * q, axis=1, keepdims=True)
        top = jnp.sqrt(jnp.maximum(square, 0.0) + 1e-06)
        if not last:
            row[...] = jnp.broadcast_to(q / top, row.shape)
            col[...] = col_next[...] / top

    center = damping + top
    rho, delta = top / center, damping / center
    zero, one = jnp.zeros_like(center), jnp.ones_like(center)

    def shifted(p):
        low = [delta * v for v in p] + [zero]
        return [a + b for a, b in zip(low, [zero] + list(p))]

    def plus(p, q, factor):
        n = max(len(p), len(q))
        p = list(p) + [zero] * (n - len(p))
        q = list(q) + [zero] * (n - len(q))
        return [a + factor * b for a, b in zip(p, q)]

    sig = one
    direction = [one]
    solution_poly = [one]
    residual = plus([one], shifted(direction), -sig)
    for sweep in range(1, ITERS):
        momentum = 0.5 * (rho * sig) ** 2 if sweep == 1 else (0.5 * rho * sig) ** 2
        sig = 1.0 / (1.0 - momentum / sig)
        direction = plus(residual, direction, momentum)
        solution_poly = plus(solution_poly, direction, sig)
        if sweep + 1 < ITERS:
            residual = plus(residual, shifted(direction), -sig)
    s0, s1, s2, s3 = solution_poly

    inverse = 1.0 / center
    y_ref[...] = full[grp_rows(grp), :] * inverse
    own_cols = pl.ds(pl.multiple_of(grp * group_ex, group_ex), group_ex)
    sc[...] = s0 * y_ref[:, own_cols]
    wide = min(256, total_ex)

    def dot_nt(a, b):
        return lax.dot_general(a, b, NT, precision=lax.Precision.HIGHEST,
                               preferred_element_type=jnp.float32)

    def solve(j, c):
        at = pl.ds(pl.multiple_of(j * wide, wide), wide)
        y_tile = y_ref[:, at]
        z_tile = dot_nt(y_ref[...], full[at, :] * inverse)
        sc[...] += dot_nt(y_tile, s1 * y_tile + s2 * z_tile) + dot_nt(z_tile, s3 * z_tile)
        return c

    lax.fori_loop(0, total_ex // wide, solve, 0)

    def score_copy(b, slot):
        start = pl.multiple_of(b * examples, examples)
        return pltpu.make_async_remote_copy(
            src_ref=sc.at[pl.ds(start, examples)], dst_ref=sc_land.at[slot],
            send_sem=s_send.at[b], recv_sem=s_recv.at[slot],
            device_id=(grp, b), device_id_type=MESH)

    def score_send(d, c):
        b = lax.rem(blk + d, blocks)
        score_copy(b, blk).start()
        return c

    lax.fori_loop(1, blocks, score_send, 0)
    sc_land[blk] = sc[pl.ds(pl.multiple_of(blk * examples, examples), examples), :]

    def score_arrive(d, c):
        b = lax.rem(blk + d, blocks)
        score_copy(b, b).wait_recv()
        return c

    lax.fori_loop(1, blocks, score_arrive, 0)
    out_ref[...] = jnp.sum(sc_land[...], axis=0) * float(examples * groups)

    def sent(d, c):
        peer, pg, pb = peer_of(d)
        feature_copy(peer, pg, pb, me).wait_send()
        stat_copy(peer, pg, pb, me).wait_send()
        return c

    lax.fori_loop(1, devices, sent, 0)
    for h in others:
        part_copy(h, grp).wait_send()
        full_copy(h, grp).wait_send()
        prow_copy(h, grp).wait_send()

    def score_sent(d, c):
        score_copy(lax.rem(blk + d, blocks), blk).wait_send()
        return c

    lax.fori_loop(1, blocks, score_sent, 0)


def shards(groups, blocks, activations, out_grads, proj_act, proj_out):
    examples = activations.shape[0] // SEQ
    rank, span = proj_act.shape[1], proj_out.shape[1]
    devices = groups * blocks
    group_ex, total_ex = examples * blocks, examples * devices
    ranks = rank // devices
    width = rank * span // blocks
    act_low = jnp.dot(activations, proj_act, preferred_element_type=jnp.float32).astype(
        jnp.bfloat16
    )
    grad_low = jnp.dot(out_grads, proj_out, preferred_element_type=jnp.float32).astype(jnp.bfloat16)
    vmem = pl.BlockSpec(memory_space=pltpu.VMEM)
    features, stat = pl.pallas_call(
        functools.partial(feature_kernel, examples),
        out_shape=(
            jax.ShapeDtypeStruct((rank * examples, span), jnp.bfloat16),
            jax.ShapeDtypeStruct((8, 128), jnp.float32),
        ),
        in_specs=[vmem] * 2,
        out_specs=(vmem, vmem),
        scratch_shapes=[pltpu.VMEM((span // 128, rank * examples, 128), jnp.float32)],
    )(act_low, grad_low)

    f32 = jnp.float32
    dma = pltpu.SemaphoreType.DMA
    return pl.pallas_call(
        functools.partial(mix_kernel, groups, blocks, examples, ranks, width),
        out_shape=jax.ShapeDtypeStruct((examples, group_ex), f32),
        in_specs=[vmem] * 2,
        out_specs=vmem,
        scratch_shapes=[
            pltpu.VMEM((devices, ranks * examples, span), jnp.bfloat16),
            pltpu.VMEM((devices, 8, 128), f32),
            pltpu.VMEM((total_ex, total_ex), f32),
            pltpu.VMEM((groups, group_ex, total_ex), f32),
            pltpu.VMEM((total_ex, total_ex), f32),
            pltpu.VMEM((8, total_ex), f32),
            pltpu.VMEM((groups, 8, total_ex), f32),
            pltpu.VMEM((8, total_ex), f32),
            pltpu.VMEM((total_ex, 128), f32),
            pltpu.VMEM((total_ex, 128), f32),
            pltpu.VMEM((group_ex, total_ex), f32),
            pltpu.VMEM((group_ex, group_ex), f32),
            pltpu.VMEM((blocks, examples, group_ex), f32),
            dma((devices,)), dma((devices,)), dma((devices,)), dma((devices,)),
            dma((groups,)), dma((groups,)), dma((groups,)), dma((groups,)),
            dma((groups,)), dma((groups,)), dma((blocks,)), dma((blocks,)),
        ],
        compiler_params=pltpu.CompilerParams(
            collective_id=0, has_side_effects=True, vmem_limit_bytes=67043328
        ),
    )(features, stat)


def solution(mesh):
    in_specs = (P(("grp", "blk"), None), P(("grp", "blk"), None), P(), P())
    out_specs = P(("grp", "blk"), None)
    body = functools.partial(shards, mesh.shape["grp"], mesh.shape["blk"])
    return jax.shard_map(body, mesh=mesh, in_specs=in_specs, out_specs=out_specs, check_vma=False)
```

time: 541 us -> 87.3 us (0.16)
  matrix products: 384 us -> 8.17 us
  Pallas kernels: 0 us -> 77.7 us
  waiting for transfers between devices: 77 us -> 0 us
  blocking collectives: 49.9 us -> 0 us
  between operations: 16.4 us -> 0.01 us
    dot_general x9 -> x0, matrix products: 378 us -> none  [the longest x3 180 us: top_estimate(): image = jnp.dot(gram_sum, vector, precision=lax.Precision.HIGHEST)]
    pallas_call x0 -> x2, Pallas kernels: none -> 77.7 us  [the longest x1 74.2 us: shards(): pl.pallas_call(functools.partial(mix_kernel, groups, blocks, examples, ra...]
    all_gather x1 -> x0, waiting for transfers between devices: 49.1 us -> none  [shards(): lax.all_gather(block_rows, 'grp', axis=0, tiled=True)]
    all_to_all x1 -> x0, blocking collectives: 32.8 us -> none  [shards(): lax.all_to_all(features, 'blk', split_axis=1, concat_axis=0, tiled=True)]
    reduce_scatter x1 -> x0, waiting for transfers between devices: 27.9 us -> none  [shards(): lax.psum_scatter(jnp.dot(block_rows, solved, preferred_element_type=jnp.f...]
    psum x1 -> x0, blocking collectives: 17.1 us -> none  [shards(): total = lax.psum(jnp.trace(gram_sum), 'blk')]
    all_to_all x3 -> x0, local copies, waits for them, and re-layouts: 5.41 us -> none  [shards(): lax.all_to_all(features, 'blk', split_axis=1, concat_axis=0, tiled=True)]
  transfers between devices with their start and end apart: 2 -> 0, of which waited for: 2 -> 0; matrix products, arithmetic and copies ran while one was open for 0% -> 0% of each run, Pallas kernels for 0% -> 0%
where the time goes in v1:
time: 87.3 us; the launch traced here: 87.1 us
  Pallas kernels  77.7 us (89%)
  matrix products  8.17 us (9%)
  local copies, waits for them, and re-layouts  1.3 us (1%)
    pallas_call x1, Pallas kernels, shards(): pl.pallas_call(functools.partial(mix_kernel, groups, blocks, examples, ra...  74.2 us
    dot_general x1, matrix products, shards(): jnp.dot(activations, proj_act, preferred_element_type=jnp.float32)  5.58 us
    pallas_call x1, Pallas kernels, shards(): pl.pallas_call(functools.partial(feature_kernel, examples), out_shape=(ja...  3.43 us
    dot_general x1, matrix products, shards(): jnp.dot(out_grads, proj_out, preferred_element_type=jnp.float32)  2.59 us

profile of v1, /device:TPU:0, one launch (start us, length us, event | category | flops | bytes accessed | tf_op | source)
XLA Modules:
  0.0 87.1 jit_solution(11416899283574603904)
XLA Ops:
  0.0 0.0 copy-start.1
  0.0 0.0 copy-start
  0.0 5.6 %convolution_convert_fusion.1.act_ref = bf16[1024,128]{1,0:T(8,128)(2,1)} fusion(bf16[1024,3072]{1,0:T(8,128)(2,1)} %param.4, bf16[3072,128]{1,0:T(8,128)(2,1)} %param.6), kind=kOutput, calls=%fused_computation.1 | convolution fusion | flops 805437440 | bytes 7340032 | tf_op jit(solution)/shard_map/dot_general | solution.py:322
  5.6 0.0 copy-done.1
  5.6 0.0 copy-done
  5.6 2.6 %convolution_convert_fusion.grad_ref = bf16[1024,256]{1,0:T(8,128)(2,1)} fusion(bf16[1024,3072]{1,0:T(8,128)(2,1)S(1)} %copy-done, bf16[3072,256]{1,0:T(8,128)(2,1)S(1)} %copy-done.1), kind=kOutput, calls=%fused_computation | convolution fusion | flops 1610874880 | bytes 8388608 | tf_op jit(solution)/shard_map/dot_general | solution.py:325
  8.2 3.4 %shard_map.46 = (bf16[2048,256]{1,0:T(8,128)(2,1)}, f32[8,128]{1,0:T(8,128)}) custom-call(bf16[1024,128]{1,0:T(8,128)(2,1)} %convolution_convert_fusion.1.act_ref, bf16[1024,256]{1,0:T(8,128)(2,1)} %convolution_convert_fusion.grad_ref), custom_call_target="tpu_custom_call" | custom-call | tf_op jit(solution)/shard_map/pallas_call | solution.py:327
  11.6 74.2 %shard_map.47 = f32[16,128]{1,0:T(8,128)} custom-call(bf16[2048,256]{1,0:T(8,128)(2,1)} %get-tuple-element.7.feat_ref, f32[8,128]{1,0:T(8,128)} %get-tuple-element.8.stat_ref), custom_call_target="tpu_custom_call" | custom-call | tf_op jit(solution)/shard_map/pallas_call | solution.py:340
  85.8 1.3 %copy.6 = f32[16,128]{1,0:T(8,128)} copy(f32[16,128]{1,0:T(8,128)} %shard_map.47) | data formatting | bytes 16384
Async XLA Ops:
  0.0 5.6 %copy-start.1 = (bf16[3072,256]{1,0:T(8,128)(2,1)S(1)}, bf16[3072,256]{1,0:T(8,128)(2,1)}, u32[]{:S(2)}) copy-start(bf16[3072,256]{1,0:T(8,128)(2,1)} %param.7) | copy-start | bytes 4718596
  0.0 5.6 %copy-start = (bf16[1024,3072]{1,0:T(8,128)(2,1)S(1)}, bf16[1024,3072]{1,0:T(8,128)(2,1)}, u32[]{:S(2)}) copy-start(bf16[1024,3072]{1,0:T(8,128)(2,1)} %param.5) | copy-start | bytes 18874372

commit v2 on v1

--- a/solution.py
+++ b/solution.py
@@ -17,33 +17,10 @@
 TN = (((0,), (0,)), ((), ()))
 
 
-def feature_kernel(examples, act_ref, grad_ref, feat_ref, stat_ref, wide):
-    rank = act_ref.shape[1]
-    for e in range(examples):
-        tokens = pl.ds(e * SEQ, SEQ)
-        product = lax.dot_general(
-            act_ref[tokens, :], grad_ref[tokens, :], TN, preferred_element_type=jnp.float32
-        )
-        for c in range(wide.shape[0]):
-            wide[c, pl.ds(e, rank, stride=examples), :] = product[:, c * 128:(c + 1) * 128]
-
-    def step(i, acc):
-        rows = pl.ds(pl.multiple_of(i * 128, 128), 128)
-        for c in range(wide.shape[0]):
-            low = wide[c, rows, :].astype(jnp.bfloat16)
-            feat_ref[rows, c * 128:(c + 1) * 128] = low
-            back = low.astype(jnp.float32)
-            acc += back * back
-        return acc
-
-    acc = lax.fori_loop(0, wide.shape[1] // 128, step, jnp.zeros((128, 128), jnp.float32))
-    stat_ref[...] = jnp.broadcast_to(jnp.sum(acc, keepdims=True), stat_ref.shape)
-
-
 def mix_kernel(
     groups, blocks, examples, ranks, width,
-    feat_ref, stat_ref, out_ref,
-    recv, stats, part, landed, full, prow_part, prow_land, row, col, col_next,
+    act_ref, grad_ref, out_ref,
+    wide, feat_ref, stat_ref, recv, stats, part, landed, packs, full, prow_part, prow_land, row, col, col_next,
     y_ref, sc, sc_land,
     f_send, f_recv, t_send, t_recv, r_send, r_recv, g_send, g_recv, p_send, p_recv, s_send, s_recv,
 ):
@@ -55,9 +32,16 @@
     grp, blk = lax.axis_index("grp"), lax.axis_index("blk")
     me = grp * blocks + blk
 
+    half = blocks // 2 * groups
+
     def peer_of(d):
-        peer = lax.rem(me + d, devices)
-        return peer, peer // blocks, lax.rem(peer, blocks)
+        pg = lax.rem(grp + lax.rem(d, groups), groups)
+        pb = lax.rem(blk + blocks // 2 + d // groups, blocks)
+        return pg * blocks + pb, pg, pb
+
+    def over_peers(step):
+        lax.fori_loop(0, half, step, 0)
+        lax.fori_loop(half + 1, devices, step, 0)
 
     barrier = pltpu.get_barrier_semaphore()
 
@@ -66,13 +50,21 @@
         pl.semaphore_signal(barrier, inc=1, device_id=(pg, pb), device_id_type=MESH)
         return c
 
-    lax.fori_loop(1, devices, greet, 0)
+    over_peers(greet)
+    for e in range(examples):
+        tokens = pl.ds(e * SEQ, SEQ)
+        product = lax.dot_general(
+            act_ref[tokens, :], grad_ref[tokens, :], TN, preferred_element_type=jnp.float32
+        )
+        for c in range(wide.shape[0]):
+            wide[c, pl.ds(e, act_ref.shape[1], stride=examples), :] = (
+                product[:, c * 128:(c + 1) * 128])
+    stat_ref[...] = jnp.zeros_like(stat_ref)
     pl.semaphore_wait(barrier, devices - 1)
 
     def feature_copy(dest, pg, pb, slot):
-        start = pl.multiple_of((pb * groups + pg) * rows_out, rows_out)
-        return pltpu.make_async_remote_copy(
-            src_ref=feat_ref.at[pl.ds(start, rows_out)], dst_ref=recv.at[slot],
+        return pltpu.make_async_remote_copy(
+            src_ref=feat_ref.at[pb * groups + pg], dst_ref=recv.at[slot],
             send_sem=f_send.at[dest], recv_sem=f_recv.at[slot],
             device_id=(pg, pb), device_id_type=MESH)
 
@@ -82,21 +74,32 @@
             send_sem=t_send.at[dest], recv_sem=t_recv.at[slot],
             device_id=(pg, pb), device_id_type=MESH)
 
+    def narrow(pg, pb):
+        slot = pb * groups + pg
+        rows = pl.ds(pl.multiple_of(slot * rows_out, rows_out), rows_out)
+        for c in range(wide.shape[0]):
+            low = wide[c, rows, :].astype(jnp.bfloat16)
+            feat_ref[slot, :, c * 128:(c + 1) * 128] = low
+            back = low.astype(jnp.float32)
+            square = jnp.sum(back * back, axis=0, keepdims=True)
+            stat_ref[...] += jnp.broadcast_to(square, stat_ref.shape)
+
     def send(d, c):
         peer, pg, pb = peer_of(d)
+        narrow(pg, pb)
         feature_copy(peer, pg, pb, me).start()
         return c
 
-    lax.fori_loop(1, devices, send, 0)
+    over_peers(send)
+    narrow(grp, blk)
+    recv[me] = feat_ref[blk * groups + grp]
 
     def send_stat(d, c):
         peer, pg, pb = peer_of(d)
         stat_copy(peer, pg, pb, me).start()
         return c
 
-    lax.fori_loop(1, devices, send_stat, 0)
-    own = pl.multiple_of((blk * groups + grp) * rows_out, rows_out)
-    recv[me] = feat_ref[pl.ds(own, rows_out), :]
+    over_peers(send_stat)
     stats[me] = stat_ref[...]
 
     def arrive(d, c):
@@ -104,33 +107,45 @@
         feature_copy(peer, pg, pb, peer).wait_recv()
         return c
 
-    lax.fori_loop(1, devices, arrive, 0)
+    over_peers(arrive)
 
     def grp_rows(h):
         return pl.ds(pl.multiple_of(h * group_ex, group_ex), group_ex)
 
-    def part_rows(h):
+    split = groups % 2 == 0
+    whole_blocks = (groups - 1) // 2 + 1
+    pair = groups // 2
+    half_ex = group_ex // 2
+
+    def block_into(h, at, left_at, left_n, right_at):
         for r in range(ranks):
             here = pl.ds(r * examples, examples)
-            left = recv[pl.ds(h * blocks, blocks), here, :].reshape(group_ex, span)
-            for c in range(groups):
-                right = recv[c * blocks:(c + 1) * blocks, here, :].reshape(group_ex, span)
-                term = lax.dot_general(left, right, NT, preferred_element_type=jnp.float32)
-                cols = slice(c * group_ex, (c + 1) * group_ex)
-                if r == 0:
-                    part[grp_rows(h), cols] = term
-                else:
-                    part[grp_rows(h), cols] += term
-
-    def part_copy(h, slot):
-        return pltpu.make_async_remote_copy(
-            src_ref=part.at[grp_rows(h)], dst_ref=landed.at[slot],
-            send_sem=r_send.at[h], recv_sem=r_recv.at[slot],
+            left = recv[pl.ds(left_at, left_n), here, :].reshape(left_n * examples, span)
+            right = recv[pl.ds(right_at, blocks), here, :].reshape(group_ex, span)
+            term = lax.dot_general(left, right, NT, preferred_element_type=jnp.float32)
+            if r == 0:
+                part[h, at:at + left_n * examples, :] = term
+            else:
+                part[h, at:at + left_n * examples, :] += term
+
+    def part_of(h):
+        for d in range(whole_blocks):
+            block_into(h, d * group_ex, h * blocks, blocks, lax.rem(h + d, groups) * blocks)
+        if split:
+            low = lax.rem(h, pair)
+            block_into(h, whole_blocks * group_ex,
+                       low * blocks + h // pair * (blocks // 2), blocks // 2,
+                       (low + pair) * blocks)
+
+    def part_copy(h, d, slot):
+        return pltpu.make_async_remote_copy(
+            src_ref=part.at[h], dst_ref=landed.at[slot],
+            send_sem=r_send.at[d], recv_sem=r_recv.at[slot],
             device_id=(h, blk), device_id_type=MESH)
 
     def full_copy(h, slot):
         return pltpu.make_async_remote_copy(
-            src_ref=full.at[grp_rows(slot)], dst_ref=full.at[grp_rows(slot)],
+            src_ref=packs.at[slot], dst_ref=packs.at[slot],
             send_sem=g_send.at[h], recv_sem=g_recv.at[slot],
             device_id=(h, blk), device_id_type=MESH)
 
@@ -144,12 +159,12 @@
 
     def part_step(d, c):
         h = lax.rem(grp + d, groups)
-        part_rows(h)
-        part_copy(h, grp).start()
+        part_of(h)
+        part_copy(h, d, groups - d - 1).start()
         return c
 
     lax.fori_loop(1, groups, part_step, 0)
-    part_rows(grp)
+    part_of(grp)
 
     ones = jnp.ones((8, span), jnp.bfloat16)
     scale = 1.0 / math.sqrt(width)
@@ -164,12 +179,12 @@
     for h in others:
         prow_copy(h, grp).start()
 
-    for h in others:
-        part_copy(h, h).wait_recv()
-    mine = part[grp_rows(grp), :]
-    for h in others:
-        mine += landed[h]
-    full[grp_rows(grp), :] = mine
+    for d, h in enumerate(others):
+        part_copy(h, d + 1, d).wait_recv()
+    mine = part[grp]
+    for d in range(groups - 1):
+        mine += landed[d]
+    packs[grp] = mine
     for h in others:
         full_copy(h, grp).start()
 
@@ -178,8 +193,8 @@
         stat_copy(peer, pg, pb, peer).wait_recv()
         return c
 
-    lax.fori_loop(1, devices, arrive_stat, 0)
-    total = jnp.sum(stats[...], axis=0)[:1, :1]
+    over_peers(arrive_stat)
+    total = jnp.sum(jnp.sum(stats[...], axis=0)[:1, :], axis=1, keepdims=True)
     damping = damping_rate * total / (width * blocks)
     for h in others:
         prow_copy(h, h).wait_recv()
@@ -189,6 +204,22 @@
     row[...] = first
     for h in others:
         full_copy(h, h).wait_recv()
+    for o in range(groups):
+        here = slice(o * group_ex, (o + 1) * group_ex)
+        for d in range(whole_blocks):
+            there = (o + d) % groups
+            there = slice(there * group_ex, (there + 1) * group_ex)
+            entry = packs[o, d * group_ex:(d + 1) * group_ex, :]
+            full[here, there] = entry
+            if d:
+                full[there, here] = entry.T
+        if split:
+            low = o % pair
+            start = low * group_ex + o // pair * half_ex
+            there = slice((low + pair) * group_ex, (low + pair + 1) * group_ex)
+            entry = packs[o, whole_blocks * group_ex:, :]
+            full[start:start + half_ex, there] = entry
+            full[there, start:start + half_ex] = entry.T
 
     tile = 128
     tiles = total_ex // tile
@@ -255,20 +286,20 @@
     y_ref[...] = full[grp_rows(grp), :] * inverse
     own_cols = pl.ds(pl.multiple_of(grp * group_ex, group_ex), group_ex)
     sc[...] = s0 * y_ref[:, own_cols]
-    wide = min(256, total_ex)
+    step_ex = min(256, total_ex)
 
     def dot_nt(a, b):
         return lax.dot_general(a, b, NT, precision=lax.Precision.HIGHEST,
                                preferred_element_type=jnp.float32)
 
     def solve(j, c):
-        at = pl.ds(pl.multiple_of(j * wide, wide), wide)
+        at = pl.ds(pl.multiple_of(j * step_ex, step_ex), step_ex)
         y_tile = y_ref[:, at]
         z_tile = dot_nt(y_ref[...], full[at, :] * inverse)
         sc[...] += dot_nt(y_tile, s1 * y_tile + s2 * z_tile) + dot_nt(z_tile, s3 * z_tile)
         return c
 
-    lax.fori_loop(0, total_ex // wide, solve, 0)
+    lax.fori_loop(0, total_ex // step_ex, solve, 0)
 
     def score_copy(b, slot):
         start = pl.multiple_of(b * examples, examples)
@@ -291,7 +322,7 @@
         return c
 
     lax.fori_loop(1, blocks, score_arrive, 0)
-    out_ref[...] = jnp.sum(sc_land[...], axis=0) * float(examples * groups)
+    out_ref[...] = jnp.sum(sc_land[...], axis=0)
 
     def sent(d, c):
         peer, pg, pb = peer_of(d)
@@ -299,9 +330,10 @@
         stat_copy(peer, pg, pb, me).wait_send()
         return c
 
-    lax.fori_loop(1, devices, sent, 0)
-    for h in others:
-        part_copy(h, grp).wait_send()
+    over_peers(sent)
+    for d, h in enumerate(others):
+        part_copy(h, d + 1, d).wait_send()
+    for h in others:
         full_copy(h, grp).wait_send()
         prow_copy(h, grp).wait_send()
 
@@ -324,29 +356,23 @@
     )
     grad_low = jnp.dot(out_grads, proj_out, preferred_element_type=jnp.float32).astype(jnp.bfloat16)
     vmem = pl.BlockSpec(memory_space=pltpu.VMEM)
-    features, stat = pl.pallas_call(
-        functools.partial(feature_kernel, examples),
-        out_shape=(
-            jax.ShapeDtypeStruct((rank * examples, span), jnp.bfloat16),
-            jax.ShapeDtypeStruct((8, 128), jnp.float32),
-        ),
-        in_specs=[vmem] * 2,
-        out_specs=(vmem, vmem),
-        scratch_shapes=[pltpu.VMEM((span // 128, rank * examples, 128), jnp.float32)],
-    )(act_low, grad_low)
-
     f32 = jnp.float32
     dma = pltpu.SemaphoreType.DMA
-    return pl.pallas_call(
+    keep = group_ex * ((groups - 1) // 2 + 1) + (0 if groups % 2 else group_ex // 2)
+    scores = pl.pallas_call(
         functools.partial(mix_kernel, groups, blocks, examples, ranks, width),
         out_shape=jax.ShapeDtypeStruct((examples, group_ex), f32),
         in_specs=[vmem] * 2,
         out_specs=vmem,
         scratch_shapes=[
+            pltpu.VMEM((span // 128, rank * examples, 128), f32),
+            pltpu.VMEM((devices, ranks * examples, span), jnp.bfloat16),
+            pltpu.VMEM((8, 128), f32),
             pltpu.VMEM((devices, ranks * examples, span), jnp.bfloat16),
             pltpu.VMEM((devices, 8, 128), f32),
-            pltpu.VMEM((total_ex, total_ex), f32),
-            pltpu.VMEM((groups, group_ex, total_ex), f32),
+            pltpu.VMEM((groups, keep, group_ex), f32),
+            pltpu.VMEM((groups - 1, keep, group_ex), f32),
+            pltpu.VMEM((groups, keep, group_ex), f32),
             pltpu.VMEM((total_ex, total_ex), f32),
             pltpu.VMEM((8, total_ex), f32),
             pltpu.VMEM((groups, 8, total_ex), f32),
@@ -363,7 +389,8 @@
         compiler_params=pltpu.CompilerParams(
             collective_id=0, has_side_effects=True, vmem_limit_bytes=67043328
         ),
-    )(features, stat)
+    )(act_low, grad_low)
+    return scores * float(examples * groups)
 
 
 def solution(mesh):

time: 87.3 us -> 71.8 us (0.82)
  Pallas kernels: 77.7 us -> 62.2 us
  other arithmetic: 0 us -> 1.3 us
  local copies, waits for them, and re-layouts: 1.3 us -> 0.01 us
    pallas_call x1, Pallas kernels: 74.2 us -> 62.2 us  [shards(): pl.pallas_call(functools.partial(mix_kernel, groups, blocks, examples, ra...]
    pallas_call x1 -> x0, Pallas kernels: 3.43 us -> none  [shards(): pl.pallas_call(functools.partial(feature_kernel, examples), out_shape=(ja...]
    mul x0 -> x1, other arithmetic: none -> 1.3 us  [shards(): return scores * float(examples * groups)]
    unnamed x5 -> x4, local copies, waits for them, and re-layouts: 1.3 us -> 0.01 us
where the time goes in v2:
time: 71.8 us; the launch traced here: 71.6 us
  Pallas kernels  62.2 us (87%)
  matrix products  8.14 us (11%)
  other arithmetic  1.3 us (2%)
    pallas_call x1, Pallas kernels, shards(): pl.pallas_call(functools.partial(mix_kernel, groups, blocks, examples, ra...  62.2 us
    dot_general x1, matrix products, shards(): jnp.dot(activations, proj_act, preferred_element_type=jnp.float32)  5.57 us
    dot_general x1, matrix products, shards(): jnp.dot(out_grads, proj_out, preferred_element_type=jnp.float32)  2.57 us

profile of v2, /device:TPU:0, one launch (start us, length us, event | category | flops | bytes accessed | tf_op | source)
XLA Modules:
  0.0 71.6 jit_solution(10311898087270098724)
XLA Ops:
  0.0 0.0 copy-start.1
  0.0 0.0 copy-start
  0.0 5.6 %convolution_convert_fusion.1.act_ref = bf16[1024,128]{1,0:T(8,128)(2,1)} fusion(bf16[1024,3072]{1,0:T(8,128)(2,1)} %param.4, bf16[3072,128]{1,0:T(8,128)(2,1)} %param.6), kind=kOutput, calls=%fused_computation.1 | convolution fusion | flops 805437440 | bytes 7340032 | tf_op jit(solution)/shard_map/dot_general | solution.py:354
  5.6 0.0 copy-done.1
  5.6 0.0 copy-done
  5.6 2.6 %convolution_convert_fusion.grad_ref = bf16[1024,256]{1,0:T(8,128)(2,1)} fusion(bf16[1024,3072]{1,0:T(8,128)(2,1)S(1)} %copy-done, bf16[3072,256]{1,0:T(8,128)(2,1)S(1)} %copy-done.1), kind=kOutput, calls=%fused_computation | convolution fusion | flops 1610874880 | bytes 8388608 | tf_op jit(solution)/shard_map/dot_general | solution.py:357
  8.1 62.2 %shard_map.46 = f32[16,128]{1,0:T(8,128)} custom-call(bf16[1024,128]{1,0:T(8,128)(2,1)} %convolution_convert_fusion.1.act_ref, bf16[1024,256]{1,0:T(8,128)(2,1)} %convolution_convert_fusion.grad_ref), custom_call_target="tpu_custom_call" | custom-call | tf_op jit(solution)/shard_map/pallas_call | solution.py:362
  70.3 1.3 %broadcast_multiply_fusion = f32[16,128]{1,0:T(8,128)} fusion(f32[16,128]{1,0:T(8,128)} %shard_map.46), kind=kLoop, calls=%fused_computation.2 | loop fusion | flops 2048 | bytes 16384 | tf_op jit(solution)/shard_map/mul | solution.py:393
Async XLA Ops:
  0.0 5.6 %copy-start.1 = (bf16[3072,256]{1,0:T(8,128)(2,1)S(1)}, bf16[3072,256]{1,0:T(8,128)(2,1)}, u32[]{:S(2)}) copy-start(bf16[3072,256]{1,0:T(8,128)(2,1)} %param.7) | copy-start | bytes 4718596
  0.0 5.6 %copy-start = (bf16[1024,3072]{1,0:T(8,128)(2,1)S(1)}, bf16[1024,3072]{1,0:T(8,128)(2,1)}, u32[]{:S(2)}) copy-start(bf16[1024,3072]{1,0:T(8,128)(2,1)} %param.5) | copy-start | bytes 18874372

commit v3 on v2

--- a/solution.py
+++ b/solution.py
@@ -128,25 +128,27 @@
             else:
                 part[h, at:at + left_n * examples, :] += term
 
-    def part_of(h):
-        for d in range(whole_blocks):
+    def part_of(h, q):
+        for d in range(1) if q == 0 else range(1, whole_blocks):
             block_into(h, d * group_ex, h * blocks, blocks, lax.rem(h + d, groups) * blocks)
-        if split:
+        if split and q == 1:
             low = lax.rem(h, pair)
             block_into(h, whole_blocks * group_ex,
                        low * blocks + h // pair * (blocks // 2), blocks // 2,
                        (low + pair) * blocks)
 
-    def part_copy(h, d, slot):
-        return pltpu.make_async_remote_copy(
-            src_ref=part.at[h], dst_ref=landed.at[slot],
-            send_sem=r_send.at[d], recv_sem=r_recv.at[slot],
+    cuts = (slice(0, group_ex), slice(group_ex, part.shape[1]))
+
+    def part_copy(h, d, slot, q):
+        return pltpu.make_async_remote_copy(
+            src_ref=part.at[h, cuts[q]], dst_ref=landed.at[slot, cuts[q]],
+            send_sem=r_send.at[2 * d + q], recv_sem=r_recv.at[2 * slot + q],
             device_id=(h, blk), device_id_type=MESH)
 
-    def full_copy(h, slot):
-        return pltpu.make_async_remote_copy(
-            src_ref=packs.at[slot], dst_ref=packs.at[slot],
-            send_sem=g_send.at[h], recv_sem=g_recv.at[slot],
+    def full_copy(h, slot, q):
+        return pltpu.make_async_remote_copy(
+            src_ref=packs.at[slot, cuts[q]], dst_ref=packs.at[slot, cuts[q]],
+            send_sem=g_send.at[2 * h + q], recv_sem=g_recv.at[2 * slot + q],
             device_id=(h, blk), device_id_type=MESH)
 
     def prow_copy(h, slot):
@@ -157,14 +159,16 @@
 
     others = [lax.rem(grp + d, groups) for d in range(1, groups)]
 
-    def part_step(d, c):
-        h = lax.rem(grp + d, groups)
-        part_of(h)
-        part_copy(h, d, groups - d - 1).start()
-        return c
-
-    lax.fori_loop(1, groups, part_step, 0)
-    part_of(grp)
+    for q in range(2):
+        def part_step(d, c, q=q):
+            h = lax.rem(grp + d, groups)
+            part_of(h, q)
+            part_copy(h, d, groups - d - 1, q).start()
+            return c
+
+        lax.fori_loop(1, groups, part_step, 0)
+    for q in range(2):
+        part_of(grp, q)
 
     ones = jnp.ones((8, span), jnp.bfloat16)
     scale = 1.0 / math.sqrt(width)
@@ -179,14 +183,15 @@
     for h in others:
         prow_copy(h, grp).start()
 
-    for d, h in enumerate(others):
-        part_copy(h, d + 1, d).wait_recv()
-    mine = part[grp]
-    for d in range(groups - 1):
-        mine += landed[d]
-    packs[grp] = mine
-    for h in others:
-        full_copy(h, grp).start()
+    for q in range(2):
+        for d, h in enumerate(others):
+            part_copy(h, d + 1, d, q).wait_recv()
+        mine = part[grp, cuts[q], :]
+        for d in range(groups - 1):
+            mine += landed[d, cuts[q], :]
+        packs[grp, cuts[q], :] = mine
+        for h in others:
+            full_copy(h, grp, q).start()
 
     def arrive_stat(d, c):
         peer, pg, pb = peer_of(d)
@@ -203,7 +208,8 @@
         first += prow_land[h]
     row[...] = first
     for h in others:
-        full_copy(h, h).wait_recv()
+        for q in range(2):
+            full_copy(h, h, q).wait_recv()
     for o in range(groups):
         here = slice(o * group_ex, (o + 1) * group_ex)
         for d in range(whole_blocks):
@@ -288,9 +294,16 @@
     sc[...] = s0 * y_ref[:, own_cols]
     step_ex = min(256, total_ex)
 
+    def halves(v):
+        high = v.astype(jnp.bfloat16)
+        return high, (v - high.astype(jnp.float32)).astype(jnp.bfloat16)
+
     def dot_nt(a, b):
-        return lax.dot_general(a, b, NT, precision=lax.Precision.HIGHEST,
-                               preferred_element_type=jnp.float32)
+        def product(x, y):
+            return lax.dot_general(x, y, NT, preferred_element_type=jnp.float32)
+
+        (a_high, a_low), (b_high, b_low) = halves(a), halves(b)
+        return product(a_high, b_high) + (product(a_high, b_low) + product(a_low, b_high))
 
     def solve(j, c):
         at = pl.ds(pl.multiple_of(j * step_ex, step_ex), step_ex)
@@ -332,9 +345,10 @@
 
     over_peers(sent)
     for d, h in enumerate(others):
-        part_copy(h, d + 1, d).wait_send()
+        for q in range(2):
+            part_copy(h, d + 1, groups - d - 2, q).wait_send()
+            full_copy(h, grp, q).wait_send()
     for h in others:
-        full_copy(h, grp).wait_send()
         prow_copy(h, grp).wait_send()
 
     def score_sent(d, c):
@@ -383,7 +397,7 @@
             pltpu.VMEM((group_ex, group_ex), f32),
             pltpu.VMEM((blocks, examples, group_ex), f32),
             dma((devices,)), dma((devices,)), dma((devices,)), dma((devices,)),
-            dma((groups,)), dma((groups,)), dma((groups,)), dma((groups,)),
+            dma((2 * groups,)), dma((2 * groups,)), dma((2 * groups,)), dma((2 * groups,)),
             dma((groups,)), dma((groups,)), dma((blocks,)), dma((blocks,)),
         ],
         compiler_params=pltpu.CompilerParams(

time: 71.8 us -> 69 us (0.961)
  Pallas kernels: 62.2 us -> 59.3 us
    pallas_call x1, Pallas kernels: 62.2 us -> 59.3 us  [shards(): pl.pallas_call(functools.partial(mix_kernel, groups, blocks, examples, ra...]
where the time goes in v3:
time: 69 us; the launch traced here: 68.7 us
  Pallas kernels  59.3 us (86%)
  matrix products  8.14 us (12%)
  other arithmetic  1.3 us (2%)
    pallas_call x1, Pallas kernels, shards(): pl.pallas_call(functools.partial(mix_kernel, groups, blocks, examples, ra...  59.3 us
    dot_general x1, matrix products, shards(): jnp.dot(activations, proj_act, preferred_element_type=jnp.float32)  5.57 us
    dot_general x1, matrix products, shards(): jnp.dot(out_grads, proj_out, preferred_element_type=jnp.float32)  2.57 us

profile of v3, /device:TPU:0, one launch (start us, length us, event | category | flops | bytes accessed | tf_op | source)
XLA Modules:
  0.0 68.7 jit_solution(7299393727477636879)
XLA Ops:
  0.0 0.0 copy-start.1
  0.0 0.0 copy-start
  0.0 5.6 %convolution_convert_fusion.1.act_ref = bf16[1024,128]{1,0:T(8,128)(2,1)} fusion(bf16[1024,3072]{1,0:T(8,128)(2,1)} %param.4, bf16[3072,128]{1,0:T(8,128)(2,1)} %param.6), kind=kOutput, calls=%fused_computation.1 | convolution fusion | flops 805437440 | bytes 7340032 | tf_op jit(solution)/shard_map/dot_general | solution.py:368
  5.6 0.0 copy-done.1
  5.6 0.0 copy-done
  5.6 2.6 %convolution_convert_fusion.grad_ref = bf16[1024,256]{1,0:T(8,128)(2,1)} fusion(bf16[1024,3072]{1,0:T(8,128)(2,1)S(1)} %copy-done, bf16[3072,256]{1,0:T(8,128)(2,1)S(1)} %copy-done.1), kind=kOutput, calls=%fused_computation | convolution fusion | flops 1610874880 | bytes 8388608 | tf_op jit(solution)/shard_map/dot_general | solution.py:371
  8.1 59.3 %shard_map.46 = f32[16,128]{1,0:T(8,128)} custom-call(bf16[1024,128]{1,0:T(8,128)(2,1)} %convolution_convert_fusion.1.act_ref, bf16[1024,256]{1,0:T(8,128)(2,1)} %convolution_convert_fusion.grad_ref), custom_call_target="tpu_custom_call" | custom-call | tf_op jit(solution)/shard_map/pallas_call | solution.py:376
  67.5 1.3 %broadcast_multiply_fusion = f32[16,128]{1,0:T(8,128)} fusion(f32[16,128]{1,0:T(8,128)} %shard_map.46), kind=kLoop, calls=%fused_computation.2 | loop fusion | flops 2048 | bytes 16384 | tf_op jit(solution)/shard_map/mul | solution.py:407
Async XLA Ops:
  0.0 5.6 %copy-start.1 = (bf16[3072,256]{1,0:T(8,128)(2,1)S(1)}, bf16[3072,256]{1,0:T(8,128)(2,1)}, u32[]{:S(2)}) copy-start(bf16[3072,256]{1,0:T(8,128)(2,1)} %param.7) | copy-start | bytes 4718596
  0.0 5.6 %copy-start = (bf16[1024,3072]{1,0:T(8,128)(2,1)S(1)}, bf16[1024,3072]{1,0:T(8,128)(2,1)}, u32[]{:S(2)}) copy-start(bf16[1024,3072]{1,0:T(8,128)(2,1)} %param.5) | copy-start | bytes 18874372

commit v4 on v3

--- a/solution.py
+++ b/solution.py
@@ -129,26 +129,27 @@
                 part[h, at:at + left_n * examples, :] += term
 
     def part_of(h, q):
-        for d in range(1) if q == 0 else range(1, whole_blocks):
-            block_into(h, d * group_ex, h * blocks, blocks, lax.rem(h + d, groups) * blocks)
-        if split and q == 1:
+        if q < whole_blocks:
+            block_into(h, q * group_ex, h * blocks, blocks, lax.rem(h + q, groups) * blocks)
+        else:
             low = lax.rem(h, pair)
             block_into(h, whole_blocks * group_ex,
                        low * blocks + h // pair * (blocks // 2), blocks // 2,
                        (low + pair) * blocks)
 
-    cuts = (slice(0, group_ex), slice(group_ex, part.shape[1]))
+    chunks = whole_blocks + int(split)
+    cuts = [slice(q * group_ex, min((q + 1) * group_ex, part.shape[1])) for q in range(chunks)]
 
     def part_copy(h, d, slot, q):
         return pltpu.make_async_remote_copy(
             src_ref=part.at[h, cuts[q]], dst_ref=landed.at[slot, cuts[q]],
-            send_sem=r_send.at[2 * d + q], recv_sem=r_recv.at[2 * slot + q],
+            send_sem=r_send.at[chunks * d + q], recv_sem=r_recv.at[chunks * slot + q],
             device_id=(h, blk), device_id_type=MESH)
 
     def full_copy(h, slot, q):
         return pltpu.make_async_remote_copy(
             src_ref=packs.at[slot, cuts[q]], dst_ref=packs.at[slot, cuts[q]],
-            send_sem=g_send.at[2 * h + q], recv_sem=g_recv.at[2 * slot + q],
+            send_sem=g_send.at[chunks * h + q], recv_sem=g_recv.at[chunks * slot + q],
             device_id=(h, blk), device_id_type=MESH)
 
     def prow_copy(h, slot):
@@ -159,7 +160,7 @@
 
     others = [lax.rem(grp + d, groups) for d in range(1, groups)]
 
-    for q in range(2):
+    for q in range(chunks):
         def part_step(d, c, q=q):
             h = lax.rem(grp + d, groups)
             part_of(h, q)
@@ -167,7 +168,7 @@
             return c
 
         lax.fori_loop(1, groups, part_step, 0)
-    for q in range(2):
+    for q in range(chunks):
         part_of(grp, q)
 
     ones = jnp.ones((8, span), jnp.bfloat16)
@@ -183,7 +184,7 @@
     for h in others:
         prow_copy(h, grp).start()
 
-    for q in range(2):
+    for q in range(chunks):
         for d, h in enumerate(others):
             part_copy(h, d + 1, d, q).wait_recv()
         mine = part[grp, cuts[q], :]
@@ -208,7 +209,7 @@
         first += prow_land[h]
     row[...] = first
     for h in others:
-        for q in range(2):
+        for q in range(chunks):
             full_copy(h, h, q).wait_recv()
     for o in range(groups):
         here = slice(o * group_ex, (o + 1) * group_ex)
@@ -345,7 +346,7 @@
 
     over_peers(sent)
     for d, h in enumerate(others):
-        for q in range(2):
+        for q in range(chunks):
             part_copy(h, d + 1, groups - d - 2, q).wait_send()
             full_copy(h, grp, q).wait_send()
     for h in others:
@@ -397,7 +398,7 @@
             pltpu.VMEM((group_ex, group_ex), f32),
             pltpu.VMEM((blocks, examples, group_ex), f32),
             dma((devices,)), dma((devices,)), dma((devices,)), dma((devices,)),
-            dma((2 * groups,)), dma((2 * groups,)), dma((2 * groups,)), dma((2 * groups,)),
+            dma((groups * groups,)), dma((groups * groups,)), dma((groups * groups,)), dma((groups * groups,)),
             dma((groups,)), dma((groups,)), dma((blocks,)), dma((blocks,)),
         ],
         compiler_params=pltpu.CompilerParams(

time: 69 us -> 69.6 us (level)
  Pallas kernels: 59.3 us -> 60 us
where the time goes in v4:
time: 69.6 us; the launch traced here: 69.4 us
  Pallas kernels  60 us (86%)
  matrix products  8.14 us (12%)
  other arithmetic  1.3 us (2%)
    pallas_call x1, Pallas kernels, shards(): pl.pallas_call(functools.partial(mix_kernel, groups, blocks, examples, ra...  60 us
    dot_general x1, matrix products, shards(): jnp.dot(activations, proj_act, preferred_element_type=jnp.float32)  5.57 us
    dot_general x1, matrix products, shards(): jnp.dot(out_grads, proj_out, preferred_element_type=jnp.float32)  2.57 us

profile of v4, /device:TPU:0, one launch (start us, length us, event | category | flops | bytes accessed | tf_op | source)
XLA Modules:
  0.0 69.4 jit_solution(6361492707851469170)
XLA Ops:
  0.0 0.0 copy-start.1
  0.0 0.0 copy-start
  0.0 5.6 %convolution_convert_fusion.1.act_ref = bf16[1024,128]{1,0:T(8,128)(2,1)} fusion(bf16[1024,3072]{1,0:T(8,128)(2,1)} %param.4, bf16[3072,128]{1,0:T(8,128)(2,1)} %param.6), kind=kOutput, calls=%fused_computation.1 | convolution fusion | flops 805437440 | bytes 7340032 | tf_op jit(solution)/shard_map/dot_general | solution.py:369
  5.6 0.0 copy-done.1
  5.6 0.0 copy-done
  5.6 2.6 %convolution_convert_fusion.grad_ref = bf16[1024,256]{1,0:T(8,128)(2,1)} fusion(bf16[1024,3072]{1,0:T(8,128)(2,1)S(1)} %copy-done, bf16[3072,256]{1,0:T(8,128)(2,1)S(1)} %copy-done.1), kind=kOutput, calls=%fused_computation | convolution fusion | flops 1610874880 | bytes 8388608 | tf_op jit(solution)/shard_map/dot_general | solution.py:372
  8.1 60.0 %shard_map.46 = f32[16,128]{1,0:T(8,128)} custom-call(bf16[1024,128]{1,0:T(8,128)(2,1)} %convolution_convert_fusion.1.act_ref, bf16[1024,256]{1,0:T(8,128)(2,1)} %convolution_convert_fusion.grad_ref), custom_call_target="tpu_custom_call" | custom-call | tf_op jit(solution)/shard_map/pallas_call | solution.py:377
  68.1 1.3 %broadcast_multiply_fusion = f32[16,128]{1,0:T(8,128)} fusion(f32[16,128]{1,0:T(8,128)} %shard_map.46), kind=kLoop, calls=%fused_computation.2 | loop fusion | flops 2048 | bytes 16384 | tf_op jit(solution)/shard_map/mul | solution.py:408
Async XLA Ops:
  0.0 5.6 %copy-start.1 = (bf16[3072,256]{1,0:T(8,128)(2,1)S(1)}, bf16[3072,256]{1,0:T(8,128)(2,1)}, u32[]{:S(2)}) copy-start(bf16[3072,256]{1,0:T(8,128)(2,1)} %param.7) | copy-start | bytes 4718596
  0.0 5.6 %copy-start = (bf16[1024,3072]{1,0:T(8,128)(2,1)S(1)}, bf16[1024,3072]{1,0:T(8,128)(2,1)}, u32[]{:S(2)}) copy-start(bf16[1024,3072]{1,0:T(8,128)(2,1)} %param.5) | copy-start | bytes 18874372
